TPU v7x, 32 devices: a whole 2x2x4 slice. The times are simulated.
32 devices in a mesh: wide: 8 (over z, y), narrow: 4 (over x, core).
Axes of the slice: x: 2, y: 2, z: 4, core: 2. Of those that a mesh axis runs over, the one named last changes fastest.
Arguments:
- layer_inputs_matrix: bfloat16 [32768, 768], P(('wide', 'narrow')), may hold values from -6 to 6
- assignment_indices: int32 [32768, 1], P(('wide', 'narrow')), may hold values from 0 to 7
- admitted_counts_matrix: int32 [8], replicated, may hold values from 24 to 48, as said below
- mixer_scaling1_factor: bfloat16 [768], P(('wide', 'narrow')), may hold values from 0.5 to 1.5
- triple_linear_matrix: bfloat16 [768, 2304], P(('wide', 'narrow')), may hold values from -0.21875 to 0.21875
- mixer_exit_matrix: bfloat16 [768, 768], P(('wide', 'narrow')), may hold values from -0.875 to 0.875
- specialist_scaling2_factor: bfloat16 [768], P(('wide', 'narrow')), may hold values from 0.5 to 1.5
- cluster_mean_columns: bfloat16 [768, 8], P(('wide', 'narrow')), may hold values from -0.21875 to 0.21875
- first_linear_matrix: bfloat16 [8, 768, 3072], P('wide', None, 'narrow'), may hold values from -0.21875 to 0.21875
- second_linear_matrix: bfloat16 [8, 768, 3072], P('wide', None, 'narrow'), may hold values from -0.109375 to 0.109375
- incoming_gradient: bfloat16 [32768, 768], P(('wide', 'narrow')), may hold values from -6 to 6
Outputs:
- mixed: bfloat16 [32768, 768], P(('wide', 'narrow'))
- tokens_grad: float32 [32768, 768], P(('wide', 'narrow'))
- norm1_gain_grad: float32 [768], P(('wide', 'narrow'))
- qkv_grad: float32 [768, 2304], P(('wide', 'narrow'))
- out_grad: float32 [768, 768], P(('wide', 'narrow'))
- norm2_gain_grad: float32 [768], P(('wide', 'narrow'))
- centroid_grad: float32 [768, 8], P(('wide', 'narrow'))
- up_grad: float32 [8, 768, 3072], P('wide', None, 'narrow')
- down_grad: float32 [8, 768, 3072], P('wide', None, 'narrow')
Inputs may be any that keep to these rules, and one draw needn't show every extreme that they name: `admitted_counts_matrix`: so a device sends at most 48 tokens to one expert.
All inputs are finite; a program needn't handle non-finite values.
Results may differ from a plain program's by a relative error of at most 0.014.
Values may be sent and summed in bfloat16 or wider, within the bound.
A program may use at most 320 MiB of HBM per device.

v0:
```python
import jax
import jax.numpy as jnp
from jax import lax
from jax.sharding import PartitionSpec as P

HD = 64
SEQ = 1024
SLOT = 48
precise = lax.Precision.HIGHEST
over_rows = (((0,), (0,)), ((), ()))
over_cols = (((1,), (1,)), ((), ()))


def layer_norm(tensor, gain_vec):
    centered = tensor - jnp.mean(tensor, -1, keepdims=True)
    spread = jnp.mean(centered * centered, -1, keepdims=True)
    return centered * lax.rsqrt(spread + 1e-05) * gain_vec


def gelu_exact(tensor):
    return jax.nn.gelu(tensor, approximate=False)


def split_heads(packed):
    seq_len = packed.shape[0]
    model_width = packed.shape[1] // 3
    head_count = model_width // HD
    queries = packed[:, :model_width].reshape(seq_len, head_count, HD)
    key_rows = packed[:, model_width : 2 * model_width].reshape(seq_len, head_count, HD)
    value_rows = packed[:, 2 * model_width :].reshape(seq_len, head_count, HD)
    raw_scores = jnp.einsum(
        "qhd,khd->hqk", queries, key_rows, preferred_element_type=jnp.float32
    ) * HD ** (-0.5)
    places = jnp.arange(seq_len)
    causal = places[:, None] >= places[None, :]
    masked = jnp.where(causal[None], raw_scores, -1e30)
    return (queries, key_rows, value_rows, masked)


def attend_forward(packed):
    queries, key_rows, value_rows, masked = split_heads(packed)
    maxima = jnp.max(masked, -1, keepdims=True)
    powers = jnp.exp(masked - maxima)
    totals = jnp.sum(powers, -1, keepdims=True)
    attn_probs = (powers / totals).astype(jnp.bfloat16)
    attended = jnp.einsum(
        "hqk,khd->qhd", attn_probs, value_rows, preferred_element_type=jnp.float32
    )
    return (attended.reshape(packed.shape[0], -1).astype(jnp.bfloat16), maxima + jnp.log(totals))


def attend_backward(member):
    packed, upstream, log_totals = member
    queries, key_rows, value_rows, masked = split_heads(packed)
    attn_probs = jnp.exp(masked - log_totals)
    probs_low = attn_probs.astype(jnp.bfloat16)
    grad_out = upstream.reshape(queries.shape)
    grad_probs = jnp.einsum(
        "qhd,khd->hqk", grad_out, value_rows, preferred_element_type=jnp.float32
    )
    grad_values = jnp.einsum(
        "hqk,qhd->khd", probs_low, grad_out, preferred_element_type=jnp.float32
    )
    grad_scores = (
        attn_probs * (grad_probs - jnp.sum(grad_probs * attn_probs, -1, keepdims=True))
    ).astype(jnp.bfloat16)
    factor = HD ** (-0.5)
    grad_queries = (
        jnp.einsum("hqk,khd->qhd", grad_scores, key_rows, preferred_element_type=jnp.float32)
        * factor
    )
    grad_keys = (
        jnp.einsum("hqk,qhd->khd", grad_scores, queries, preferred_element_type=jnp.float32)
        * factor
    )
    seq_len = packed.shape[0]
    joined = jnp.concatenate(
        [
            grad_queries.reshape(seq_len, -1),
            grad_keys.reshape(seq_len, -1),
            grad_values.reshape(seq_len, -1),
        ],
        1,
    )
    return joined.astype(jnp.bfloat16)


def expert_rows(row_block, up_mat, down_mat):
    pre_act = jnp.dot(row_block, up_mat, preferred_element_type=jnp.float32)
    hidden = gelu_exact(pre_act).astype(jnp.bfloat16)
    return lax.dot_general(hidden, down_mat, over_cols, preferred_element_type=jnp.float32)


def expert_grads(row_block, grad_block, up_mat, down_mat):
    pre_act = jnp.dot(row_block, up_mat, preferred_element_type=jnp.float32)
    hidden, gelu_back = jax.vjp(gelu_exact, pre_act)
    hidden_low = hidden.astype(jnp.bfloat16)
    down_part = lax.dot_general(
        grad_block, hidden_low, over_rows, preferred_element_type=jnp.float32
    )
    grad_hidden = jnp.dot(grad_block, down_mat, preferred_element_type=jnp.float32)
    grad_pre = gelu_back(grad_hidden)[0].astype(jnp.bfloat16)
    up_part = lax.dot_general(row_block, grad_pre, over_rows, preferred_element_type=jnp.float32)
    return (grad_pre, up_part, down_part)


def fill_slots(row_vals, target, slot_count):
    buffer = jnp.zeros((slot_count + 1, row_vals.shape[1]), row_vals.dtype).at[target].set(row_vals)
    return buffer[:slot_count]


def read_slots(buffer, target):
    padded = jnp.concatenate([buffer, jnp.zeros((1, buffer.shape[1]), buffer.dtype)], 0)
    return padded[target]


def shards(
    layer_inputs_matrix,
    assignment_indices,
    admitted_counts_matrix,
    mixer_scaling1_factor,
    triple_linear_matrix,
    mixer_exit_matrix,
    specialist_scaling2_factor,
    cluster_mean_columns,
    first_linear_matrix,
    second_linear_matrix,
    incoming_gradient,
):
    gain_one, qkv_mat, out_mat, gain_two, centers = (
        lax.all_gather(mixer_scaling1_factor, ("wide", "narrow"), axis=0, tiled=True),
        lax.all_gather(triple_linear_matrix, ("wide", "narrow"), axis=0, tiled=True),
        lax.all_gather(mixer_exit_matrix, ("wide", "narrow"), axis=0, tiled=True),
        lax.all_gather(specialist_scaling2_factor, ("wide", "narrow"), axis=0, tiled=True),
        lax.all_gather(cluster_mean_columns, ("wide", "narrow"), axis=0, tiled=True),
    )
    gain_one = gain_one.astype(jnp.float32)
    gain_two = gain_two.astype(jnp.float32)
    centers = centers.astype(jnp.float32)
    token_rows = layer_inputs_matrix.astype(jnp.float32)
    tok_count, model_width = layer_inputs_matrix.shape
    seq_count = tok_count // SEQ
    normed, norm1_back = jax.vjp(layer_norm, token_rows, gain_one)
    normed_low = normed.astype(jnp.bfloat16)
    qkv_rows = jnp.dot(normed_low, qkv_mat, preferred_element_type=jnp.float32).astype(jnp.bfloat16)
    packed_seqs = qkv_rows.reshape(seq_count, SEQ, 3 * model_width)
    attended, log_totals = lax.map(attend_forward, packed_seqs)
    attended = attended.reshape(tok_count, model_width)
    residual = token_rows + jnp.dot(attended, out_mat, preferred_element_type=jnp.float32)
    normed_two, norm2_back = jax.vjp(layer_norm, residual, gain_two)
    sent_rows = normed_two.astype(jnp.bfloat16)
    dispatched_items = assignment_indices[:, 0]
    specialist_overall_sum = admitted_counts_matrix.shape[0]
    slot_count = specialist_overall_sum * SLOT
    specialist_indicator = (
        dispatched_items[:, None] == jnp.arange(specialist_overall_sum, dtype=jnp.int32)[None, :]
    ).astype(jnp.int32)
    before = jnp.cumsum(specialist_indicator, 0) - specialist_indicator
    ranked = jnp.sum(before * specialist_indicator, 1)
    position_ceilings = jnp.sum(specialist_indicator * admitted_counts_matrix[None, :], 1)
    retained_couple_filter = ranked < position_ceilings
    target = jnp.where(retained_couple_filter, dispatched_items * SLOT + ranked, slot_count)
    kept_rows = retained_couple_filter.astype(jnp.float32)
    choose = specialist_indicator.astype(jnp.float32)
    send_buf = fill_slots(sent_rows, target, slot_count).reshape(
        specialist_overall_sum, SLOT, model_width
    )
    local_rows = lax.all_to_all(send_buf, "wide", split_axis=0, concat_axis=0, tiled=True).reshape(
        slot_count, model_width
    )
    gathered = lax.all_gather(local_rows, "narrow", axis=0, tiled=True)
    expert_local = lax.psum_scatter(
        expert_rows(gathered, first_linear_matrix[0], second_linear_matrix[0]).astype(jnp.bfloat16),
        "narrow",
        scatter_dimension=0,
        tiled=True,
    )
    returned = lax.all_to_all(
        expert_local.reshape(specialist_overall_sum, SLOT, model_width),
        "wide",
        split_axis=0,
        concat_axis=0,
        tiled=True,
    )
    expert_tok = read_slots(returned.reshape(slot_count, model_width), target).astype(jnp.float32)
    center_rows = lax.dot_general(choose, centers, over_cols, precision=precise)
    logits = jnp.sum(normed_two * center_rows, 1)
    sigma = jax.nn.sigmoid(logits)
    gating = sigma * kept_rows
    mixed = (residual + gating[:, None] * expert_tok).astype(jnp.bfloat16)
    grad_y = incoming_gradient.astype(jnp.float32)
    grad_logit = jnp.sum(grad_y * expert_tok, 1) * sigma * (1.0 - sigma) * kept_rows
    grad_normed = grad_logit[:, None] * center_rows
    centroid_part = lax.dot_general(
        normed_two, choose * grad_logit[:, None], over_rows, precision=precise
    )
    grad_expert = (grad_y * gating[:, None]).astype(jnp.bfloat16)
    grad_buf = fill_slots(grad_expert, target, slot_count).reshape(
        specialist_overall_sum, SLOT, model_width
    )
    grad_local = lax.all_to_all(grad_buf, "wide", split_axis=0, concat_axis=0, tiled=True).reshape(
        slot_count, model_width
    )
    grad_gathered = lax.all_gather(grad_local, "narrow", axis=0, tiled=True)
    grad_pre, up_part, down_part = expert_grads(
        gathered, grad_gathered, first_linear_matrix[0], second_linear_matrix[0]
    )
    input_back = lax.psum_scatter(
        lax.dot_general(
            grad_pre, first_linear_matrix[0], over_cols, preferred_element_type=jnp.float32
        ).astype(jnp.bfloat16),
        "narrow",
        scatter_dimension=0,
        tiled=True,
    )
    up_grad = up_part[None]
    down_grad = down_part[None]
    back_rows = lax.all_to_all(
        input_back.reshape(specialist_overall_sum, SLOT, model_width),
        "wide",
        split_axis=0,
        concat_axis=0,
        tiled=True,
    )
    grad_normed = grad_normed + read_slots(
        back_rows.reshape(slot_count, model_width), target
    ).astype(jnp.float32)
    grad_resid_norm, gain_two_part = norm2_back(grad_normed)
    grad_resid = grad_y + grad_resid_norm
    grad_branch = grad_resid.astype(jnp.bfloat16)
    out_part = lax.dot_general(attended, grad_branch, over_rows, preferred_element_type=jnp.float32)
    grad_attended = lax.dot_general(
        grad_branch, out_mat, over_cols, preferred_element_type=jnp.float32
    ).astype(jnp.bfloat16)
    grad_packed = lax.map(
        attend_backward,
        (packed_seqs, grad_attended.reshape(seq_count, SEQ, model_width), log_totals),
    )
    grad_packed = grad_packed.reshape(tok_count, 3 * model_width)
    qkv_part = lax.dot_general(
        normed_low, grad_packed, over_rows, preferred_element_type=jnp.float32
    )
    grad_normed_one = lax.dot_general(
        grad_packed, qkv_mat, over_cols, preferred_element_type=jnp.float32
    )
    grad_token_norm, gain_one_part = norm1_back(grad_normed_one)
    tokens_grad = grad_resid + grad_token_norm
    gain_one_grad, qkv_grad, out_grad, gain_two_grad, centroid_grad = (
        lax.psum_scatter(gain_one_part, ("wide", "narrow"), scatter_dimension=0, tiled=True),
        lax.psum_scatter(qkv_part, ("wide", "narrow"), scatter_dimension=0, tiled=True),
        lax.psum_scatter(out_part, ("wide", "narrow"), scatter_dimension=0, tiled=True),
        lax.psum_scatter(gain_two_part, ("wide", "narrow"), scatter_dimension=0, tiled=True),
        lax.psum_scatter(centroid_part, ("wide", "narrow"), scatter_dimension=0, tiled=True),
    )
    return (
        mixed,
        tokens_grad,
        gain_one_grad,
        qkv_grad,
        out_grad,
        gain_two_grad,
        centroid_grad,
        up_grad,
        down_grad,
    )


def solution(mesh):
    in_specs = (
        P(("wide", "narrow"), None),
        P(("wide", "narrow"), None),
        P(),
        P(("wide", "narrow")),
        P(("wide", "narrow"), None),
        P(("wide", "narrow"), None),
        P(("wide", "narrow")),
        P(("wide", "narrow"), None),
        P("wide", None, "narrow"),
        P("wide", None, "narrow"),
        P(("wide", "narrow"), None),
    )
    out_specs = (
        P(("wide", "narrow"), None),
        P(("wide", "narrow"), None),
        P(("wide", "narrow")),
        P(("wide", "narrow"), None),
        P(("wide", "narrow"), None),
        P(("wide", "narrow")),
        P(("wide", "narrow"), None),
        P("wide", None, "narrow"),
        P("wide", None, "narrow"),
    )
    return jax.shard_map(shards, mesh=mesh, in_specs=in_specs, out_specs=out_specs, check_vma=False)
```

profile of v0, /device:TPU:0, one launch (start us, length us, event | category | flops | bytes accessed | tf_op | source)
XLA Modules:
  0.0 762.4 jit_solution(11529941645791292390)
XLA Ops:
  10.8 42.0 %all-reduce.8 = (bf16[768]{0:T(1024)(128)(2,1)S(1)}, bf16[768]{0:T(1024)(128)(2,1)S(1)}) all-reduce(bf16[768]{0:T(1024)(128)(2,1)S(1)} %dynamic-update-slice, bf16[768]{0:T(1024)(128)(2,1)S(1)} %dynamic-update-slice.1), channel_id=1, replica_groups=mesh['wide'=8,'narrow'=4] {'wide','narrow'}, use_global_device_ids=true, to_apply=%add.2 | all-reduce | flops 1536 | bytes 6144
  56.3 40.8 %all-gather = bf16[32,24,8]{1,2,0:T(8,128)(2,1)S(1)} all-gather(bf16[1,24,8]{1,2,0:T(8,128)(2,1)} %bitcast.122), channel_id=1, replica_groups=mesh['wide'=8,'narrow'=4] {'wide','narrow'}, dimensions={0}, use_global_device_ids=true | all-gather | bytes 12672 | tf_op jit(solution)/shard_map/all_gather | solution.py:135
  103.6 6.5 convolution_convert_fusion
  115.1 2.7 copy.54
  120.4 21.5 %fusion.6 = (f32[12,1024]{1,0:T(8,128)S(1)}, f32[12,1024,1024]{1,2,0:T(8,128)}) fusion(pred[1024,1024]{0,1:T(8,128)(4,1)S(1)} %iota_compare_fusion, bf16[1024,12,64]{0,2,1:T(8,128)(2,1)} %bitcast.92, bf16[1024,12,64]{0,2,1:T(8,128)(2,1)} %bitcast.94), kind=kOutput, calls=%fused_computation.15 | convolution fusion | flops 1648349184 | bytes 54575104 | tf_op jit(solution)/shard_map/while/body/eval_jaxpr/qhd,khd->hqk/dot_general | solution.py:31
  141.9 21.0 %fusion = f32[12,1024]{1,0:T(8,128)S(1)} fusion(f32[12,1024]{1,0:T(8,128)S(1)} %get-tuple-element.86, f32[12,1024,1024]{1,2,0:T(8,128)} %get-tuple-element.87, pred[1024,1024]{0,1:T(8,128)(4,1)S(1)} %iota_compare_fusion), kind=kLoop, calls=%fused_computation.10 | loop fusion | flops 50319360 | bytes 51478528 | tf_op jit(solution)/shard_map/while/body/eval_jaxpr/reduce_sum | solution.py:44
  162.9 21.9 %fusion.36 = bf16[12,64,1024]{2,1,0:T(8,128)(2,1)} fusion(bf16[1024,12,64]{0,2,1:T(8,128)(2,1)S(1)} %bitcast.97, f32[12,1024]{1,0:T(8,128)S(1)} %fusion, f32[12,1024]{1,0:T(8,128)S(1)} %get-tuple-element.86, f32[12,1024,1024]{1,2,0:T(8,128)} %get-tuple-element.87, pred[1024,1024]{0,1:T(8,128)(4,1)S(1)} %iota_compare_fusion), kind=kOutput, calls=%fused_computation.80 | convolution fusion | flops 1674313728 | bytes 54624256 | tf_op jit(solution)/shard_map/while/body/eval_jaxpr/hqk,khd->qhd/dot_general | solution.py:46
  184.9 3.8 fusion.75
  189.1 4.8 multiply_reduce_fusion.3
  196.4 5.8 scatter_custom_fusion
  202.3 20.3 %all_to_all.20 = bf16[8,48,768]{2,1,0:T(8,128)(2,1)} all-to-all(bf16[8,48,768]{2,1,0:T(8,128)(2,1)S(1)} %bitcast.104), channel_id=1, replica_groups=mesh['wide'=8,'narrow'=4] {'wide'}, dimensions={0} | all-to-all | bytes 1179648 | tf_op jit(solution)/shard_map/all_to_all | solution.py:168
  222.7 21.7 %all-gather.10.cloned.1.call-done = bf16[1536,768]{1,0:T(8,128)(2,1)} async-done(((bf16[384,768]{1,0:T(8,128)(2,1)}), bf16[1536,768]{1,0:T(8,128)(2,1)}) %all-gather.10.cloned.1.call-update) | async-done | bytes 2359312 | tf_op jit(solution)/shard_map/all_gather | solution.py:171
  244.4 14.4 %multiply_convert_fusion.1 = (bf16[1536,768]{1,0:T(8,128)(2,1)S(1)}, f32[1536,768]{1,0:T(8,128)}, f32[1536,768]{1,0:T(8,128)}) fusion(bf16[1536,768]{1,0:T(8,128)(2,1)} %all-gather.10.cloned.1.call-done, bf16[1,768,768]{2,1,0:T(8,128)(2,1)S(1)} %copy-done), kind=kOutput, calls=%fused_computation.33 | convolution fusion | flops 1888616448 | bytes 15335424 | tf_op jit(solution)/shard_map/dot_general | solution.py:89
  260.2 4.7 convolution_convert_fusion.2
  264.9 33.2 %reduce-scatter.6.cloned.1.call-done = bf16[384,768]{1,0:T(8,128)(2,1)} async-done(((bf16[1536,768]{1,0:T(8,128)(2,1)}), bf16[384,768]{1,0:T(8,128)(2,1)}) %reduce-scatter.6.cloned.1.call-update) | async-done | bytes 589840 | tf_op jit(solution)/shard_map/reduce_scatter | solution.py:172
  298.2 5.5 all-to-all-start.1
  303.7 2.7 copy.60
  307.0 12.6 %all-to-all-done.1 = bf16[8,48,768]{2,1,0:T(8,128)(2,1)S(1)} async-done(((bf16[8,48,768]{2,1,0:T(8,128)(2,1)}), bf16[8,48,768]{2,1,0:T(8,128)(2,1)S(1)}, u32[]{:S(2)}, u32[]{:S(2)}) %all-to-all-start.1) | async-done | bytes 589856 | tf_op jit(solution)/shard_map/all_to_all | solution.py:178
  319.6 5.5 gather_fusion
  327.7 2.6 fusion.25
  334.5 5.8 scatter_custom_fusion.1
  340.4 20.2 %all_to_all.21 = bf16[8,48,768]{2,1,0:T(8,128)(2,1)} all-to-all(bf16[8,48,768]{2,1,0:T(8,128)(2,1)S(1)} %bitcast.105), channel_id=1, replica_groups=mesh['wide'=8,'narrow'=4] {'wide'}, dimensions={0} | all-to-all | bytes 1179648 | tf_op jit(solution)/shard_map/all_to_all | solution.py:201
  360.9 21.5 %all-gather.12.cloned.1.call-done = bf16[1536,768]{1,0:T(8,128)(2,1)} async-done(((bf16[384,768]{1,0:T(8,128)(2,1)}), bf16[1536,768]{1,0:T(8,128)(2,1)}) %all-gather.12.cloned.1.call-update) | async-done | bytes 2359312 | tf_op jit(solution)/shard_map/all_gather | solution.py:204
  382.4 7.9 %add_convert_fusion = bf16[1536,768]{1,0:T(8,128)(2,1)S(1)} fusion(f32[1536,768]{1,0:T(8,128)} %get-tuple-element.79, f32[1536,768]{1,0:T(8,128)} %get-tuple-element.91, bf16[1536,768]{1,0:T(8,128)(2,1)} %all-gather.12.cloned.1.call-done, bf16[1,768,768]{2,1,0:T(8,128)(2,1)} %param.20), kind=kOutput, calls=%fused_computation.32 | convolution fusion | flops 1828454400 | bytes 15335424 | tf_op jit(solution)/shard_map/dot_general | solution.py:101
  391.6 3.5 convolution_convert_fusion.1
  395.1 33.2 %reduce-scatter.8.cloned.1.call-done = bf16[384,768]{1,0:T(8,128)(2,1)} async-done(((bf16[1536,768]{1,0:T(8,128)(2,1)}), bf16[384,768]{1,0:T(8,128)(2,1)}) %reduce-scatter.8.cloned.1.call-update) | async-done | bytes 589840 | tf_op jit(solution)/shard_map/reduce_scatter | solution.py:208
  428.3 5.5 all-to-all-start.3
  433.9 15.8 %all-to-all-done.3 = bf16[8,48,768]{2,1,0:T(8,128)(2,1)S(1)} async-done(((bf16[8,48,768]{2,1,0:T(8,128)(2,1)}), bf16[8,48,768]{2,1,0:T(8,128)(2,1)S(1)}, u32[]{:S(2)}, u32[]{:S(2)}) %all-to-all-start.3) | async-done | bytes 589856 | tf_op jit(solution)/shard_map/all_to_all | solution.py:218
  449.8 5.2 gather_fusion.1
  455.0 2.6 copy.62
  457.7 5.3 multiply_reduce_fusion.1
  463.2 4.1 fusion.72
  470.1 2.9 fusion.76
  472.9 3.2 convolution_convert_fusion.3
  477.2 20.8 %fusion.33 = bf16[12,64,1024]{2,1,0:T(8,128)(2,1)} fusion(bf16[1024,12,64]{0,2,1:T(8,128)(2,1)S(1)} %bitcast.108, f32[12,1024]{1,0:T(8,128)S(1)} %log_add_fusion, f32[12,1024,1024]{1,2,0:T(8,128)} %get-tuple-element.87, pred[1024,1024]{0,1:T(8,128)(4,1)S(1)} %iota_compare_fusion), kind=kOutput, calls=%fused_computation.76 | convolution fusion | flops 1661730816 | bytes 54575104 | tf_op jit(solution)/shard_map/while/body/eval_jaxpr/hqk,qhd->khd/dot_general | solution.py:61
  498.1 34.6 %multiply_reduce_fusion = (f32[12,1024]{1,0:T(8,128)S(1)}, f32[12,1024,1024]{1,2,0:T(8,128)}) fusion(f32[12,1024]{1,0:T(8,128)S(1)} %log_add_fusion, f32[12,1024,1024]{1,2,0:T(8,128)} %get-tuple-element.87, pred[1024,1024]{0,1:T(8,128)(4,1)S(1)} %iota_compare_fusion, bf16[1024,12,64]{0,2,1:T(8,128)(2,1)} %bitcast.109, bf16[1024,12,64]{0,2,1:T(8,128)(2,1)} %bitcast.96), kind=kOutput, calls=%fused_computation.5 | convolution fusion | flops 1673515008 | bytes 104955904 | tf_op jit(solution)/shard_map/while/body/eval_jaxpr/qhd,khd->hqk/dot_general | solution.py:58
  532.7 42.1 %multiply_convert_fusion = bf16[12,1024,1024]{1,2,0:T(8,128)(2,1)} fusion(f32[12,1024,1024]{1,2,0:T(8,128)} %get-tuple-element.93, f32[12,1024]{1,0:T(8,128)S(1)} %get-tuple-element.92, f32[12,1024]{1,0:T(8,128)S(1)} %log_add_fusion, f32[12,1024,1024]{1,2,0:T(8,128)} %get-tuple-element.87, pred[1024,1024]{0,1:T(8,128)(4,1)S(1)} %iota_compare_fusion), kind=kLoop, calls=%fused_computation.4 | loop fusion | flops 75497472 | bytes 126976000 | tf_op jit(solution)/shard_map/while/body/eval_jaxpr/convert_element_type | solution.py:66
  574.8 14.4 %multiply_convert_fusion.2 = bf16[12,64,1024]{2,1,0:T(8,128)(2,1)} fusion(bf16[1024,12,64]{0,2,1:T(8,128)(2,1)} %bitcast.93, bf16[12,1024,1024]{1,2,0:T(8,128)(2,1)} %multiply_convert_fusion), kind=kOutput, calls=%fused_computation.63 | convolution fusion | flops 1612185600 | bytes 28311552 | tf_op jit(solution)/shard_map/while/body/eval_jaxpr/hqk,qhd->khd/dot_general | solution.py:73
  589.2 13.4 %multiply_convert_fusion.3 = bf16[12,64,1024]{2,1,0:T(8,128)(2,1)S(1)} fusion(bf16[1024,12,64]{0,2,1:T(8,128)(2,1)} %bitcast.95, bf16[12,1024,1024]{1,2,0:T(8,128)(2,1)} %multiply_convert_fusion), kind=kOutput, calls=%fused_computation.64 | convolution fusion | flops 1612185600 | bytes 28311552 | tf_op jit(solution)/shard_map/while/body/eval_jaxpr/hqk,khd->qhd/dot_general | solution.py:69
  603.9 6.9 fusion.31
  611.5 5.0 fusion.27
  616.5 5.3 convolution_bitcast_fusion
  621.8 3.7 convolution_bitcast_fusion.1
  628.1 6.9 fusion.24
  638.0 38.4 %all-reduce.7 = (f32[768]{0:T(1024)S(1)}, f32[768]{0:T(1024)S(1)}, f32[768,8]{0,1:T(8,128)S(1)}) all-reduce(f32[768]{0:T(1024)S(1)} %get-tuple-element.65, f32[768]{0:T(1024)S(1)} %copy-done.43, f32[768,8]{0,1:T(8,128)S(1)} %fusion.27), channel_id=4, replica_groups=mesh['wide'=8,'narrow'=4] {'wide','narrow'}, use_global_device_ids=true, to_apply=%region_22.23.clone | all-reduce | flops 7680 | bytes 61440
  677.6 6.6 add_add_fusion.2
  684.2 3.6 copy.67
  688.4 66.9 %reduce-scatter.10.cloned.1.call-done = f32[24,2304]{1,0:T(8,128)} async-done(((f32[768,2304]{1,0:T(8,128)}), f32[24,2304]{1,0:T(8,128)}) %reduce-scatter.10.cloned.1.call-update) | async-done | bytes 221200 | tf_op jit(solution)/shard_map/reduce_scatter | solution.py:250
  (166 shorter events, 48.2 us)
Async XLA Ops:
  7.2 237.2 %copy-start = (bf16[1,768,768]{2,1,0:T(8,128)(2,1)S(1)}, bf16[1,768,768]{2,1,0:T(8,128)(2,1)}, u32[]{:S(2)}) copy-start(bf16[1,768,768]{2,1,0:T(8,128)(2,1)} %param.19) | copy-start | bytes 3538948
  7.2 96.4 %all-gather.6.cloned.1.call-start = ((), (), s32[]{:S(2)}) async-start(), calls=%async_computation.8 | async-start | bytes 3649536 | tf_op jit(solution)/shard_map/all_gather | solution.py:132
  7.9 176.9 %all-gather.8.cloned.1.call-start = ((), (), s32[]{:S(2)}) async-start(), calls=%async_computation.9 | async-start | bytes 1216512 | tf_op jit(solution)/shard_map/all_gather | solution.py:133
  8.7 235.7 %all-gather.10.cloned.1.call-start = ((), (), s32[]{:S(2)}) async-start(), calls=%async_computation.10 | async-start | bytes 2949120 | tf_op jit(solution)/shard_map/all_gather | solution.py:171
  52.8 50.8 %copy-start.29 = (f32[768]{0:T(1024)}, f32[768]{0:T(1024)S(1)}, u32[]{:S(2)}) copy-start(f32[768]{0:T(1024)S(1)} %convert_element_type.89) | copy-start | bytes 9220
  52.8 136.3 %copy-start.21 = (f32[768]{0:T(1024)}, f32[768]{0:T(1024)S(1)}, u32[]{:S(2)}) copy-start(f32[768]{0:T(1024)S(1)} %convert_element_type.98) | copy-start | bytes 9220
  97.2 6.2 copy-start.25
  97.2 6.2 copy-start.46
  101.5 8.7 %copy-start.27 = (f32[1024]{0:T(1024)}, f32[1024]{0:T(1024)S(1)}, u32[]{:S(2)}) copy-start(f32[1024]{0:T(1024)S(1)} %broadcast_multiply_fusion.1) | copy-start | bytes 12292
  103.4 6.8 copy-start.33
  103.4 6.8 copy-start.31
  103.5 6.7 copy-start.38
  103.5 6.7 copy-start.40
  103.5 92.9 %copy-start.44 = (s32[1024,1]{0,1:T(1,128)}, s32[1024,1]{0,1:T(1,128)S(1)}, u32[]{:S(2)}) copy-start(s32[1024,1]{0,1:T(1,128)S(1)} %compare_select_fusion) | copy-start | bytes 12292
  141.9 21.0 %copy-start.11 = (bf16[1024,768]{0,1:T(8,128)(2,1)S(1)}, bf16[1024,768]{0,1:T(8,128)(2,1)}, u32[]{:S(2)}) copy-start(bf16[1024,768]{0,1:T(8,128)(2,1)} %copy.53) | copy-start | bytes 4718596
  188.6 5.2 copy-start.2
  189.1 4.8 copy-start.35
  189.1 4.8 copy-start.23
  222.7 75.5 %reduce-scatter.6.cloned.1.call-start = ((), (), s32[]{:S(2)}) async-start(), calls=%async_computation.11 | async-start | bytes 2949120 | tf_op jit(solution)/shard_map/reduce_scatter | solution.py:172
  264.9 41.5 %copy-start.45 = (s32[1024,1]{0,1:T(1,128)S(1)}, s32[1024,1]{0,1:T(1,128)}, u32[]{:S(2)}) copy-start(s32[1024,1]{0,1:T(1,128)} %copy-done.44) | copy-start | bytes 12292
  298.2 21.4 %all-to-all-start.1 = ((bf16[8,48,768]{2,1,0:T(8,128)(2,1)}), bf16[8,48,768]{2,1,0:T(8,128)(2,1)S(1)}, u32[]{:S(2)}, u32[]{:S(2)}) async-start(bf16[8,48,768]{2,1,0:T(8,128)(2,1)} %bitcast.111), calls=%async_computation.2 | async-start | bytes 1179648 | tf_op jit(solution)/shard_map/all_to_all | solution.py:178
  303.7 78.7 %all-gather.12.cloned.1.call-start = ((), (), s32[]{:S(2)}) async-start(), calls=%async_computation.12 | async-start | bytes 2949120 | tf_op jit(solution)/shard_map/all_gather | solution.py:204
  325.1 5.2 copy-start.37
  325.1 5.2 copy-start.39
  325.1 5.2 copy-start.41
  360.6 67.7 %reduce-scatter.8.cloned.1.call-start = ((), (), s32[]{:S(2)}) async-start(), calls=%async_computation.13 | async-start | bytes 2949120 | tf_op jit(solution)/shard_map/reduce_scatter | solution.py:208
  395.1 54.7 %copy-start.42 = (s32[1024]{0:T(1024)S(1)}, s32[1024]{0:T(1024)}, u32[]{:S(2)}) copy-start(s32[1024]{0:T(1024)} %broadcast_clamp_fusion) | copy-start | bytes 12292
  428.3 21.4 %all-to-all-start.3 = ((bf16[8,48,768]{2,1,0:T(8,128)(2,1)}), bf16[8,48,768]{2,1,0:T(8,128)(2,1)S(1)}, u32[]{:S(2)}, u32[]{:S(2)}) async-start(bf16[8,48,768]{2,1,0:T(8,128)(2,1)} %bitcast.110), calls=%async_computation.5 | async-start | bytes 1179648 | tf_op jit(solution)/shard_map/all_to_all | solution.py:218
  433.8 254.6 %reduce-scatter.12.cloned.1.call-start = ((), (), s32[]{:S(2)}) async-start(), calls=%async_computation.15 | async-start | bytes 2433024 | tf_op jit(solution)/shard_map/reduce_scatter | solution.py:251
  457.6 5.3 copy-start.36
  457.6 5.3 copy-start.3
  457.6 5.3 copy-start.7
  457.6 5.6 copy-start.9
  463.2 4.1 copy-start.6
  467.3 2.8 copy-start.47
  532.7 222.7 %reduce-scatter.10.cloned.1.call-start = ((), (), s32[]{:S(2)}) async-start(), calls=%async_computation.14 | async-start | bytes 7299072 | tf_op jit(solution)/shard_map/reduce_scatter | solution.py:250
  589.2 14.6 %copy-start.4 = (bf16[1024,768]{0,1:T(8,128)(2,1)S(1)}, bf16[1024,768]{0,1:T(8,128)(2,1)}, u32[]{:S(2)}) copy-start(bf16[1024,768]{0,1:T(8,128)(2,1)} %copy.52) | copy-start | bytes 4718596
  589.2 14.6 %copy-start.12 = (bf16[12,64,1024]{2,1,0:T(8,128)(2,1)S(1)}, bf16[12,64,1024]{2,1,0:T(8,128)(2,1)}, u32[]{:S(2)}) copy-start(bf16[12,64,1024]{2,1,0:T(8,128)(2,1)} %multiply_convert_fusion.2) | copy-start | bytes 4718596
  589.2 14.6 %copy-start.28 = (f32[1024]{0:T(1024)S(1)}, f32[1024]{0:T(1024)}, u32[]{:S(2)}) copy-start(f32[1024]{0:T(1024)} %copy-done.27) | copy-start | bytes 12292
  589.2 14.6 %copy-start.30 = (f32[768]{0:T(1024)S(1)}, f32[768]{0:T(1024)}, u32[]{:S(2)}) copy-start(f32[768]{0:T(1024)} %copy-done.29) | copy-start | bytes 9220
  589.2 14.6 %copy-start.32 = (f32[1024]{0:T(1024)S(1)}, f32[1024]{0:T(1024)}, u32[]{:S(2)}) copy-start(f32[1024]{0:T(1024)} %copy-done.31) | copy-start | bytes 12292
  589.2 14.6 %copy-start.48 = (bf16[12,64,1024]{2,1,0:T(8,128)(2,1)S(1)}, bf16[12,64,1024]{2,1,0:T(8,128)(2,1)}, u32[]{:S(2)}) copy-start(bf16[12,64,1024]{2,1,0:T(8,128)(2,1)} %fusion.33) | copy-start | bytes 4718596
  611.5 5.0 copy-start.15
  616.5 5.3 copy-start.13
  616.5 5.3 copy-start.17
  628.1 6.9 copy-start.34
  635.0 3.0 copy-start.43
  677.6 77.7 %copy-start.1 = (bf16[1,768,768]{2,1,0:T(8,128)(2,1)S(1)}, bf16[1,768,768]{2,1,0:T(8,128)(2,1)}, u32[]{:S(2)}) copy-start(bf16[1,768,768]{2,1,0:T(8,128)(2,1)} %param.19) | copy-start | bytes 3538948
  (11 other events, 18.3 us)
Sparse Core Ops, SparseCore 0:
  10.9 62.9 all-gather.5
  76.8 52.8 all-gather.7
  222.8 21.5 all-gather.9
  265.1 33.0 reduce-scatter.5
  360.8 21.5 all-gather.11
  395.2 33.0 reduce-scatter.7
  532.8 97.1 reduce-scatter.11
  637.2 118.0 reduce-scatter.9
where the time goes:
time: 773 us; the launch traced here: 762 us
  waiting for transfers between devices  206 us (27%)
  matrix products  206 us (27%)
  blocking collectives  162 us (21%)
  other arithmetic  93.3 us (12%)
  local copies, waits for them, and re-layouts  68.3 us (9%)
  between operations  15 us (2%)
  starting transfers between devices  11.6 us (2%)
    unnamed x2, blocking collectives  80.5 us
    reduce_scatter x1, waiting for transfers between devices, shards(): lax.psum_scatter(qkv_part, ('wide', 'narrow'), scatter_dimension=0, tiled...  66.9 us
    convert_element_type x1, other arithmetic, attend_backward(): grad_scores = (attn_probs * (grad_probs - jnp.sum(grad_probs * attn_probs...  42.1 us
    all_gather x1, blocking collectives, shards(): lax.all_gather(cluster_mean_columns, ('wide', 'narrow'), axis=0, tiled=True)  40.8 us
    dot_general x1, matrix products, attend_backward(): jnp.einsum('qhd,khd->hqk', grad_out, value_rows, preferred_element_type=j...  34.6 us
    reduce_scatter x1, waiting for transfers between devices, shards(): lax.psum_scatter(expert_rows(gathered, first_linear_matrix[0], second_lin...  33.2 us
    reduce_scatter x1, waiting for transfers between devices, shards(): lax.psum_scatter(lax.dot_general(grad_pre, first_linear_matrix[0], over_c...  33.2 us
    unnamed x110, local copies, waits for them, and re-layouts  25.1 us
  transfers between devices with their start and end apart: 10, of which 7 were waited for; matrix products, arithmetic and copies ran while one was open for 28% of the time, Pallas kernels for 0%

commit v1 on v0

--- a/solution.py
+++ b/solution.py
@@ -168,7 +168,14 @@
     local_rows = lax.all_to_all(send_buf, "wide", split_axis=0, concat_axis=0, tiled=True).reshape(
         slot_count, model_width
     )
-    gathered = lax.all_gather(local_rows, "narrow", axis=0, tiled=True)
+    ring = [local_rows]
+    for hop in range(3):
+        ring.append(lax.ppermute(ring[-1], "narrow", [(dev, (dev + 1) % 4) for dev in range(4)]))
+    gathered = jnp.roll(
+        jnp.concatenate(ring[::-1], axis=0),
+        (lax.axis_index("narrow") + 1) * ring[0].shape[0],
+        axis=0,
+    )
     expert_local = lax.psum_scatter(
         expert_rows(gathered, first_linear_matrix[0], second_linear_matrix[0]).astype(jnp.bfloat16),
         "narrow",

time: 773 us -> 779 us (level)
    ppermute x0 -> x3, waiting for transfers between devices: none -> 28.3 us  [shards(): lax.ppermute(ring[-1], 'narrow', [(dev, (dev + 1) % 4) for dev in range(4)])]
    all_gather x1 -> x0, waiting for transfers between devices: 21.7 us -> none  [shards(): gathered = lax.all_gather(local_rows, 'narrow', axis=0, tiled=True)]
    unnamed x110 -> x121, local copies, waits for them, and re-layouts: 25.1 us -> 29.8 us
  transfers between devices with their start and end apart: 10 -> 12, of which waited for: 7 -> 9; matrix products, arithmetic and copies ran while one was open for 28% -> 27% of each run, Pallas kernels for 0% -> 0%
where the time goes in v1:
time: 779 us; the launch traced here: 768 us
  waiting for transfers between devices  210 us (27%)
  matrix products  204 us (26%)
  blocking collectives  161 us (21%)
  other arithmetic  93.3 us (12%)
  local copies, waits for them, and re-layouts  73.1 us (9%)
  between operations  15.1 us (2%)
  starting transfers between devices  11.5 us (1%)
    unnamed x2, blocking collectives  80.5 us
    reduce_scatter x1, waiting for transfers between devices, shards(): lax.psum_scatter(qkv_part, ('wide', 'narrow'), scatter_dimension=0, tiled...  66.6 us
    convert_element_type x1, other arithmetic, attend_backward(): grad_scores = (attn_probs * (grad_probs - jnp.sum(grad_probs * attn_probs...  42.1 us
    all_gather x1, blocking collectives, shards(): lax.all_gather(cluster_mean_columns, ('wide', 'narrow'), axis=0, tiled=True)  40.8 us
    dot_general x1, matrix products, attend_backward(): jnp.einsum('qhd,khd->hqk', grad_out, value_rows, preferred_element_type=j...  34.6 us
    reduce_scatter x1, waiting for transfers between devices, shards(): lax.psum_scatter(lax.dot_general(grad_pre, first_linear_matrix[0], over_c...  33.2 us
    reduce_scatter x1, waiting for transfers between devices, shards(): lax.psum_scatter(expert_rows(gathered, first_linear_matrix[0], second_lin...  30.7 us
    unnamed x121, local copies, waits for them, and re-layouts  29.8 us
  transfers between devices with their start and end apart: 12, of which 9 were waited for; matrix products, arithmetic and copies ran while one was open for 27% of the time, Pallas kernels for 0%

profile of v1, /device:TPU:0, one launch (start us, length us, event | category | flops | bytes accessed | tf_op | source)
XLA Modules:
  0.0 768.1 jit_solution(712965665701724383)
XLA Ops:
  10.8 42.0 %all-reduce.8 = (bf16[768]{0:T(1024)(128)(2,1)S(1)}, bf16[768]{0:T(1024)(128)(2,1)S(1)}) all-reduce(bf16[768]{0:T(1024)(128)(2,1)S(1)} %dynamic-update-slice, bf16[768]{0:T(1024)(128)(2,1)S(1)} %dynamic-update-slice.1), channel_id=1, replica_groups=mesh['wide'=8,'narrow'=4] {'wide','narrow'}, use_global_device_ids=true, to_apply=%add.2 | all-reduce | flops 1536 | bytes 6144
  56.3 40.8 %all-gather = bf16[32,24,8]{1,2,0:T(8,128)(2,1)S(1)} all-gather(bf16[1,24,8]{1,2,0:T(8,128)(2,1)} %bitcast.122), channel_id=1, replica_groups=mesh['wide'=8,'narrow'=4] {'wide','narrow'}, dimensions={0}, use_global_device_ids=true | all-gather | bytes 12672 | tf_op jit(solution)/shard_map/all_gather | solution.py:135
  103.6 6.5 convolution_convert_fusion
  112.4 2.7 copy.55
  115.1 2.7 copy.54
  120.4 21.5 %fusion.6 = (f32[12,1024]{1,0:T(8,128)S(1)}, f32[12,1024,1024]{1,2,0:T(8,128)}) fusion(pred[1024,1024]{0,1:T(8,128)(4,1)S(1)} %iota_compare_fusion, bf16[1024,12,64]{0,2,1:T(8,128)(2,1)} %bitcast.90, bf16[1024,12,64]{0,2,1:T(8,128)(2,1)} %bitcast.92), kind=kOutput, calls=%fused_computation.15 | convolution fusion | flops 1648349184 | bytes 54575104 | tf_op jit(solution)/shard_map/while/body/eval_jaxpr/qhd,khd->hqk/dot_general | solution.py:31
  141.9 21.0 %fusion = f32[12,1024]{1,0:T(8,128)S(1)} fusion(f32[12,1024]{1,0:T(8,128)S(1)} %get-tuple-element.86, f32[12,1024,1024]{1,2,0:T(8,128)} %get-tuple-element.87, pred[1024,1024]{0,1:T(8,128)(4,1)S(1)} %iota_compare_fusion), kind=kLoop, calls=%fused_computation.10 | loop fusion | flops 50319360 | bytes 51478528 | tf_op jit(solution)/shard_map/while/body/eval_jaxpr/reduce_sum | solution.py:44
  162.9 22.0 %fusion.43 = bf16[12,64,1024]{2,1,0:T(8,128)(2,1)} fusion(bf16[1024,12,64]{0,2,1:T(8,128)(2,1)S(1)} %bitcast.95, f32[12,1024]{1,0:T(8,128)S(1)} %fusion, f32[12,1024]{1,0:T(8,128)S(1)} %get-tuple-element.86, f32[12,1024,1024]{1,2,0:T(8,128)} %get-tuple-element.87, pred[1024,1024]{0,1:T(8,128)(4,1)S(1)} %iota_compare_fusion), kind=kOutput, calls=%fused_computation.84 | convolution fusion | flops 1674313728 | bytes 54624256 | tf_op jit(solution)/shard_map/while/body/eval_jaxpr/hqk,khd->qhd/dot_general | solution.py:46
  184.9 3.8 fusion.83
  189.2 4.8 multiply_reduce_fusion.3
  196.5 5.8 scatter_custom_fusion
  202.4 19.6 %all_to_all.20 = bf16[8,48,768]{2,1,0:T(8,128)(2,1)S(1)} all-to-all(bf16[8,48,768]{2,1,0:T(8,128)(2,1)S(1)} %bitcast.104), channel_id=1, replica_groups=mesh['wide'=8,'narrow'=4] {'wide'}, dimensions={0} | all-to-all | bytes 1179648 | tf_op jit(solution)/shard_map/all_to_all | solution.py:168
  222.0 9.3 %collective-permute-done = bf16[384,768]{1,0:T(8,128)(2,1)S(1)} collective-permute-done((bf16[384,768]{1,0:T(8,128)(2,1)S(1)}, bf16[384,768]{1,0:T(8,128)(2,1)S(1)}, u32[]{:S(2)}, u32[]{:S(2)}) %collective-permute-start) | collective-permute-done | bytes 589856 | tf_op jit(solution)/shard_map/ppermute | solution.py:173
  231.3 9.4 %collective-permute-done.1 = bf16[384,768]{1,0:T(8,128)(2,1)} collective-permute-done((bf16[384,768]{1,0:T(8,128)(2,1)S(1)}, bf16[384,768]{1,0:T(8,128)(2,1)}, u32[]{:S(2)}, u32[]{:S(2)}) %collective-permute-start.1) | collective-permute-done | bytes 589856 | tf_op jit(solution)/shard_map/ppermute | solution.py:173
  240.7 9.6 %collective-permute-done.2 = bf16[384,768]{1,0:T(8,128)(2,1)} collective-permute-done((bf16[384,768]{1,0:T(8,128)(2,1)}, bf16[384,768]{1,0:T(8,128)(2,1)}, u32[]{:S(2)}, u32[]{:S(2)}) %collective-permute-start.2) | collective-permute-done | bytes 589856 | tf_op jit(solution)/shard_map/ppermute | solution.py:173
  255.0 13.2 %multiply_convert_fusion.1 = (bf16[1536,768]{1,0:T(8,128)(2,1)S(1)}, f32[1536,768]{1,0:T(8,128)}, f32[1536,768]{1,0:T(8,128)}) fusion(bf16[1,768,768]{2,1,0:T(8,128)(2,1)S(1)} %copy-done, bf16[3072,768]{1,0:T(8,128)(2,1)S(1)} %constant_dynamic-update-slice_fusion, s32[]{:T(128)S(6)} %select_n.36), kind=kOutput, calls=%fused_computation.33 | convolution fusion | flops 1888616448 | bytes 15335428 | tf_op jit(solution)/shard_map/dot_general | solution.py:89
  269.7 3.5 convolution_convert_fusion.2
  273.2 30.7 %reduce-scatter.6.cloned.1.call-done = bf16[384,768]{1,0:T(8,128)(2,1)} async-done(((bf16[1536,768]{1,0:T(8,128)(2,1)}), bf16[384,768]{1,0:T(8,128)(2,1)}) %reduce-scatter.6.cloned.1.call-update) | async-done | bytes 589840 | tf_op jit(solution)/shard_map/reduce_scatter | solution.py:179
  303.8 5.5 all-to-all-start.1
  312.6 12.7 %all-to-all-done.1 = bf16[8,48,768]{2,1,0:T(8,128)(2,1)S(1)} async-done(((bf16[8,48,768]{2,1,0:T(8,128)(2,1)}), bf16[8,48,768]{2,1,0:T(8,128)(2,1)S(1)}, u32[]{:S(2)}, u32[]{:S(2)}) %all-to-all-start.1) | async-done | bytes 589856 | tf_op jit(solution)/shard_map/all_to_all | solution.py:185
  325.3 5.5 gather_fusion
  340.2 5.8 scatter_custom_fusion.1
  346.1 20.2 %all_to_all.21 = bf16[8,48,768]{2,1,0:T(8,128)(2,1)} all-to-all(bf16[8,48,768]{2,1,0:T(8,128)(2,1)S(1)} %bitcast.105), channel_id=1, replica_groups=mesh['wide'=8,'narrow'=4] {'wide'}, dimensions={0} | all-to-all | bytes 1179648 | tf_op jit(solution)/shard_map/all_to_all | solution.py:208
  366.6 21.5 %all-gather.9.cloned.1.call-done = bf16[1536,768]{1,0:T(8,128)(2,1)} async-done(((bf16[384,768]{1,0:T(8,128)(2,1)}), bf16[1536,768]{1,0:T(8,128)(2,1)}) %all-gather.9.cloned.1.call-update) | async-done | bytes 2359312 | tf_op jit(solution)/shard_map/all_gather | solution.py:211
  388.0 7.9 %add_convert_fusion = bf16[1536,768]{1,0:T(8,128)(2,1)S(1)} fusion(f32[1536,768]{1,0:T(8,128)} %get-tuple-element.79, f32[1536,768]{1,0:T(8,128)} %get-tuple-element.91, bf16[1536,768]{1,0:T(8,128)(2,1)} %all-gather.9.cloned.1.call-done, bf16[1,768,768]{2,1,0:T(8,128)(2,1)} %param.20), kind=kOutput, calls=%fused_computation.32 | convolution fusion | flops 1828454400 | bytes 15335424 | tf_op jit(solution)/shard_map/dot_general | solution.py:101
  397.3 3.5 convolution_convert_fusion.1
  400.8 33.2 %reduce-scatter.8.cloned.1.call-done = bf16[384,768]{1,0:T(8,128)(2,1)} async-done(((bf16[1536,768]{1,0:T(8,128)(2,1)}), bf16[384,768]{1,0:T(8,128)(2,1)}) %reduce-scatter.8.cloned.1.call-update) | async-done | bytes 589840 | tf_op jit(solution)/shard_map/reduce_scatter | solution.py:215
  434.0 5.5 all-to-all-start.3
  439.6 15.8 %all-to-all-done.3 = bf16[8,48,768]{2,1,0:T(8,128)(2,1)S(1)} async-done(((bf16[8,48,768]{2,1,0:T(8,128)(2,1)}), bf16[8,48,768]{2,1,0:T(8,128)(2,1)S(1)}, u32[]{:S(2)}, u32[]{:S(2)}) %all-to-all-start.3) | async-done | bytes 589856 | tf_op jit(solution)/shard_map/all_to_all | solution.py:225
  455.5 5.2 gather_fusion.1
  463.4 5.3 multiply_reduce_fusion.1
  468.9 4.0 fusion.80
  475.7 2.9 fusion.84
  478.7 3.1 convolution_convert_fusion.3
  483.0 20.8 %fusion.37 = bf16[12,64,1024]{2,1,0:T(8,128)(2,1)} fusion(bf16[1024,12,64]{0,2,1:T(8,128)(2,1)S(1)} %bitcast.108, f32[12,1024]{1,0:T(8,128)S(1)} %log_add_fusion, f32[12,1024,1024]{1,2,0:T(8,128)} %get-tuple-element.87, pred[1024,1024]{0,1:T(8,128)(4,1)S(1)} %iota_compare_fusion), kind=kOutput, calls=%fused_computation.80 | convolution fusion | flops 1661730816 | bytes 54575104 | tf_op jit(solution)/shard_map/while/body/eval_jaxpr/hqk,qhd->khd/dot_general | solution.py:61
  503.7 34.6 %multiply_reduce_fusion = (f32[12,1024]{1,0:T(8,128)S(1)}, f32[12,1024,1024]{1,2,0:T(8,128)}) fusion(f32[12,1024]{1,0:T(8,128)S(1)} %log_add_fusion, f32[12,1024,1024]{1,2,0:T(8,128)} %get-tuple-element.87, pred[1024,1024]{0,1:T(8,128)(4,1)S(1)} %iota_compare_fusion, bf16[1024,12,64]{0,2,1:T(8,128)(2,1)} %bitcast.109, bf16[1024,12,64]{0,2,1:T(8,128)(2,1)} %bitcast.94), kind=kOutput, calls=%fused_computation.5 | convolution fusion | flops 1673515008 | bytes 104955904 | tf_op jit(solution)/shard_map/while/body/eval_jaxpr/qhd,khd->hqk/dot_general | solution.py:58
  538.4 42.1 %multiply_convert_fusion = bf16[12,1024,1024]{1,2,0:T(8,128)(2,1)} fusion(f32[12,1024,1024]{1,2,0:T(8,128)} %get-tuple-element.93, f32[12,1024]{1,0:T(8,128)S(1)} %get-tuple-element.92, f32[12,1024]{1,0:T(8,128)S(1)} %log_add_fusion, f32[12,1024,1024]{1,2,0:T(8,128)} %get-tuple-element.87, pred[1024,1024]{0,1:T(8,128)(4,1)S(1)} %iota_compare_fusion), kind=kLoop, calls=%fused_computation.4 | loop fusion | flops 75497472 | bytes 126976000 | tf_op jit(solution)/shard_map/while/body/eval_jaxpr/convert_element_type | solution.py:66
  580.5 14.4 %multiply_convert_fusion.2 = bf16[12,64,1024]{2,1,0:T(8,128)(2,1)} fusion(bf16[1024,12,64]{0,2,1:T(8,128)(2,1)} %bitcast.91, bf16[12,1024,1024]{1,2,0:T(8,128)(2,1)} %multiply_convert_fusion), kind=kOutput, calls=%fused_computation.63 | convolution fusion | flops 1612185600 | bytes 28311552 | tf_op jit(solution)/shard_map/while/body/eval_jaxpr/hqk,qhd->khd/dot_general | solution.py:73
  594.9 13.4 %multiply_convert_fusion.3 = bf16[12,64,1024]{2,1,0:T(8,128)(2,1)S(1)} fusion(bf16[1024,12,64]{0,2,1:T(8,128)(2,1)} %bitcast.93, bf16[12,1024,1024]{1,2,0:T(8,128)(2,1)} %multiply_convert_fusion), kind=kOutput, calls=%fused_computation.64 | convolution fusion | flops 1612185600 | bytes 28311552 | tf_op jit(solution)/shard_map/while/body/eval_jaxpr/hqk,khd->qhd/dot_general | solution.py:69
  609.6 6.9 fusion.35
  617.2 5.0 fusion.27
  622.3 5.4 fusion.40
  627.6 3.7 convolution_bitcast_fusion
  634.0 6.9 fusion.24
  643.8 38.5 %all-reduce.7 = (f32[768]{0:T(1024)S(1)}, f32[768]{0:T(1024)S(1)}, f32[768,8]{0,1:T(8,128)S(1)}) all-reduce(f32[768]{0:T(1024)S(1)} %get-tuple-element.65, f32[768]{0:T(1024)S(1)} %copy-done.44, f32[768,8]{0,1:T(8,128)S(1)} %fusion.27), channel_id=4, replica_groups=mesh['wide'=8,'narrow'=4] {'wide','narrow'}, use_global_device_ids=true, to_apply=%region_22.23.clone | all-reduce | flops 7680 | bytes 61440
  683.5 6.6 add_add_fusion.2
  690.0 3.7 copy.67
  694.4 66.6 %reduce-scatter.10.cloned.1.call-done = f32[24,2304]{1,0:T(8,128)} async-done(((f32[768,2304]{1,0:T(8,128)}), f32[24,2304]{1,0:T(8,128)}) %reduce-scatter.10.cloned.1.call-update) | async-done | bytes 221200 | tf_op jit(solution)/shard_map/reduce_scatter | solution.py:257
  (181 shorter events, 58.1 us)
Async XLA Ops:
  7.2 247.8 %copy-start = (bf16[1,768,768]{2,1,0:T(8,128)(2,1)S(1)}, bf16[1,768,768]{2,1,0:T(8,128)(2,1)}, u32[]{:S(2)}) copy-start(bf16[1,768,768]{2,1,0:T(8,128)(2,1)} %param.19) | copy-start | bytes 3538948
  7.2 96.4 %all-gather.5.cloned.1.call-start = ((), (), s32[]{:S(2)}) async-start(), calls=%async_computation.8 | async-start | bytes 3649536 | tf_op jit(solution)/shard_map/all_gather | solution.py:132
  7.9 177.0 %all-gather.7.cloned.1.call-start = ((), (), s32[]{:S(2)}) async-start(), calls=%async_computation.9 | async-start | bytes 1216512 | tf_op jit(solution)/shard_map/all_gather | solution.py:133
  8.7 295.2 %reduce-scatter.6.cloned.1.call-start = ((), (), s32[]{:S(2)}) async-start(), calls=%async_computation.10 | async-start | bytes 2949120 | tf_op jit(solution)/shard_map/reduce_scatter | solution.py:179
  52.8 50.8 %copy-start.30 = (f32[768]{0:T(1024)}, f32[768]{0:T(1024)S(1)}, u32[]{:S(2)}) copy-start(f32[768]{0:T(1024)S(1)} %convert_element_type.89) | copy-start | bytes 9220
  52.8 136.4 %copy-start.22 = (f32[768]{0:T(1024)}, f32[768]{0:T(1024)S(1)}, u32[]{:S(2)}) copy-start(f32[768]{0:T(1024)S(1)} %convert_element_type.98) | copy-start | bytes 9220
  97.2 6.2 copy-start.26
  97.2 6.2 copy-start.47
  101.5 8.6 %copy-start.28 = (f32[1024]{0:T(1024)}, f32[1024]{0:T(1024)S(1)}, u32[]{:S(2)}) copy-start(f32[1024]{0:T(1024)S(1)} %broadcast_multiply_fusion.1) | copy-start | bytes 12292
  103.3 6.8 copy-start.34
  103.4 6.8 copy-start.32
  103.5 6.7 copy-start.39
  103.5 6.7 copy-start.41
  103.5 93.0 %copy-start.45 = (s32[1024,1]{0,1:T(1,128)}, s32[1024,1]{0,1:T(1,128)S(1)}, u32[]{:S(2)}) copy-start(s32[1024,1]{0,1:T(1,128)S(1)} %compare_select_fusion) | copy-start | bytes 12292
  141.9 21.0 %copy-start.11 = (bf16[1024,768]{0,1:T(8,128)(2,1)S(1)}, bf16[1024,768]{0,1:T(8,128)(2,1)}, u32[]{:S(2)}) copy-start(bf16[1024,768]{0,1:T(8,128)(2,1)} %copy.53) | copy-start | bytes 4718596
  188.7 5.2 copy-start.2
  189.1 4.8 copy-start.36
  222.0 9.3 %collective-permute-start = (bf16[384,768]{1,0:T(8,128)(2,1)S(1)}, bf16[384,768]{1,0:T(8,128)(2,1)S(1)}, u32[]{:S(2)}, u32[]{:S(2)}) collective-permute-start(bf16[384,768]{1,0:T(8,128)(2,1)S(1)} %bitcast.96), channel_id=1, source_target_pairs={{0,1},{1,2},{2,3},{3,0},{4,5},{5,6},{6,7},{7,4},{8,9},{9,10},{10,1... | collective-permute-start | bytes 1769480 | tf_op jit(solution)/shard_map/ppermute | solution.py:173
  231.3 9.4 %collective-permute-start.1 = (bf16[384,768]{1,0:T(8,128)(2,1)S(1)}, bf16[384,768]{1,0:T(8,128)(2,1)}, u32[]{:S(2)}, u32[]{:S(2)}) collective-permute-start(bf16[384,768]{1,0:T(8,128)(2,1)S(1)} %collective-permute-done), channel_id=1, source_target_pairs={{0,1},{1,2},{2,3},{3,0},{4,5},{5,6},{6,7},{7,4},{8,9},{9,10},{10,1... | collective-permute-start | bytes 1769480 | tf_op jit(solution)/shard_map/ppermute | solution.py:173
  240.7 9.6 %collective-permute-start.2 = (bf16[384,768]{1,0:T(8,128)(2,1)}, bf16[384,768]{1,0:T(8,128)(2,1)}, u32[]{:S(2)}, u32[]{:S(2)}) collective-permute-start(bf16[384,768]{1,0:T(8,128)(2,1)} %collective-permute-done.1), channel_id=1, source_target_pairs={{0,1},{1,2},{2,3},{3,0},{4,5},{5,6},{6,7},{7,4},{8,9},{9,10},{10,1... | collective-permute-start | bytes 1769480 | tf_op jit(solution)/shard_map/ppermute | solution.py:173
  255.0 13.2 %copy-start.18 = (bf16[3072,768]{1,0:T(8,128)(2,1)}, bf16[3072,768]{1,0:T(8,128)(2,1)S(1)}, u32[]{:S(2)}) copy-start(bf16[3072,768]{1,0:T(8,128)(2,1)S(1)} %constant_dynamic-update-slice_fusion) | copy-start | bytes 14155780
  255.0 14.7 %copy-start.48 = (bf16[1,768,768]{2,1,0:T(8,128)(2,1)S(1)}, bf16[1,768,768]{2,1,0:T(8,128)(2,1)}, u32[]{:S(2)}) copy-start(bf16[1,768,768]{2,1,0:T(8,128)(2,1)} %param.20) | copy-start | bytes 3538948
  273.1 38.9 %copy-start.46 = (s32[1024,1]{0,1:T(1,128)S(1)}, s32[1024,1]{0,1:T(1,128)}, u32[]{:S(2)}) copy-start(s32[1024,1]{0,1:T(1,128)} %copy-done.45) | copy-start | bytes 12292
  303.8 21.4 %all-to-all-start.1 = ((bf16[8,48,768]{2,1,0:T(8,128)(2,1)}), bf16[8,48,768]{2,1,0:T(8,128)(2,1)S(1)}, u32[]{:S(2)}, u32[]{:S(2)}) async-start(bf16[8,48,768]{2,1,0:T(8,128)(2,1)} %bitcast.111), calls=%async_computation.2 | async-start | bytes 1179648 | tf_op jit(solution)/shard_map/all_to_all | solution.py:185
  309.4 78.7 %all-gather.9.cloned.1.call-start = ((), (), s32[]{:S(2)}) async-start(), calls=%async_computation.11 | async-start | bytes 2949120 | tf_op jit(solution)/shard_map/all_gather | solution.py:211
  330.8 5.3 copy-start.38
  330.8 5.3 copy-start.40
  330.8 5.3 copy-start.42
  366.3 67.7 %reduce-scatter.8.cloned.1.call-start = ((), (), s32[]{:S(2)}) async-start(), calls=%async_computation.12 | async-start | bytes 2949120 | tf_op jit(solution)/shard_map/reduce_scatter | solution.py:215
  400.8 54.7 %copy-start.43 = (s32[1024]{0:T(1024)S(1)}, s32[1024]{0:T(1024)}, u32[]{:S(2)}) copy-start(s32[1024]{0:T(1024)} %broadcast_clamp_fusion) | copy-start | bytes 12292
  434.0 21.4 %all-to-all-start.3 = ((bf16[8,48,768]{2,1,0:T(8,128)(2,1)}), bf16[8,48,768]{2,1,0:T(8,128)(2,1)S(1)}, u32[]{:S(2)}, u32[]{:S(2)}) async-start(bf16[8,48,768]{2,1,0:T(8,128)(2,1)} %bitcast.110), calls=%async_computation.5 | async-start | bytes 1179648 | tf_op jit(solution)/shard_map/all_to_all | solution.py:225
  439.5 254.9 %reduce-scatter.12.cloned.1.call-start = ((), (), s32[]{:S(2)}) async-start(), calls=%async_computation.14 | async-start | bytes 2433024 | tf_op jit(solution)/shard_map/reduce_scatter | solution.py:258
  463.3 5.3 copy-start.37
  463.3 5.3 copy-start.3
  463.3 5.3 copy-start.7
  463.3 5.6 copy-start.9
  538.3 222.7 %reduce-scatter.10.cloned.1.call-start = ((), (), s32[]{:S(2)}) async-start(), calls=%async_computation.13 | async-start | bytes 7299072 | tf_op jit(solution)/shard_map/reduce_scatter | solution.py:257
  594.9 14.7 %copy-start.4 = (bf16[1024,768]{0,1:T(8,128)(2,1)S(1)}, bf16[1024,768]{0,1:T(8,128)(2,1)}, u32[]{:S(2)}) copy-start(bf16[1024,768]{0,1:T(8,128)(2,1)} %copy.52) | copy-start | bytes 4718596
  594.9 14.7 %copy-start.12 = (bf16[12,64,1024]{2,1,0:T(8,128)(2,1)S(1)}, bf16[12,64,1024]{2,1,0:T(8,128)(2,1)}, u32[]{:S(2)}) copy-start(bf16[12,64,1024]{2,1,0:T(8,128)(2,1)} %multiply_convert_fusion.2) | copy-start | bytes 4718596
  594.9 14.7 %copy-start.29 = (f32[1024]{0:T(1024)S(1)}, f32[1024]{0:T(1024)}, u32[]{:S(2)}) copy-start(f32[1024]{0:T(1024)} %copy-done.28) | copy-start | bytes 12292
  594.9 14.7 %copy-start.31 = (f32[768]{0:T(1024)S(1)}, f32[768]{0:T(1024)}, u32[]{:S(2)}) copy-start(f32[768]{0:T(1024)} %copy-done.30) | copy-start | bytes 9220
  594.9 14.7 %copy-start.33 = (f32[1024]{0:T(1024)S(1)}, f32[1024]{0:T(1024)}, u32[]{:S(2)}) copy-start(f32[1024]{0:T(1024)} %copy-done.32) | copy-start | bytes 12292
  594.9 14.7 %copy-start.50 = (bf16[12,64,1024]{2,1,0:T(8,128)(2,1)S(1)}, bf16[12,64,1024]{2,1,0:T(8,128)(2,1)}, u32[]{:S(2)}) copy-start(bf16[12,64,1024]{2,1,0:T(8,128)(2,1)} %fusion.37) | copy-start | bytes 4718596
  617.2 5.0 copy-start.17
  622.2 5.4 copy-start.14
  622.3 5.4 copy-start.15
  634.0 6.9 copy-start.35
  683.5 77.6 %copy-start.1 = (bf16[1,768,768]{2,1,0:T(8,128)(2,1)S(1)}, bf16[1,768,768]{2,1,0:T(8,128)(2,1)}, u32[]{:S(2)}) copy-start(bf16[1,768,768]{2,1,0:T(8,128)(2,1)} %param.19) | copy-start | bytes 3538948
  (15 other events, 32.9 us)
Sparse Core Ops, SparseCore 0:
  10.9 62.8 all-gather.4
  76.7 52.9 all-gather.6
  273.3 30.5 reduce-scatter.5
  366.4 21.5 all-gather.8
  400.9 33.0 reduce-scatter.7
  538.4 97.1 reduce-scatter.11
  642.8 118.1 reduce-scatter.9
